TPU v7x, 32 devices: a whole 2x2x4 slice. The times are simulated.
32 devices in a mesh: row: 4 (over y, x), col: 4 (over z), depth: 2 (over core).
Axes of the slice: x: 2, y: 2, z: 4, core: 2. Of those that a mesh axis runs over, the one named last changes fastest.
Arguments:
- a_blocks: bfloat16 [32, 32, 2, 128, 128], P(('row', 'col', 'depth')), may hold values from -1.25 to 1.25
- a_columns: int32 [32, 32, 2], P(('row', 'col', 'depth')), may hold values from 0 to 319, as said below
- a_live: int32 [32, 32, 2], P(('row', 'col', 'depth')), may hold values from 0 to 1
- atom_rows: int32 [32], P(('row', 'col', 'depth')), may hold values from 0 to 31, as said below
- b_blocks: bfloat16 [320, 4, 6, 128, 128], P(('row', 'depth'), 'col'), may hold values from -1.25 to 1.25
- b_columns: int32 [320, 4, 6], P(('row', 'depth'), 'col'), may hold values from 0 to 319, as said below
- b_live: int32 [320, 4, 6], P(('row', 'depth'), 'col'), may hold values from 0 to 1, as said below
- c_columns: int32 [32, 4, 8], P('row', 'col'), may hold values from 0 to 319, as said below
- c_live: int32 [32, 4, 8], P('row', 'col'), may hold values from 0 to 1
Outputs:
- product: bfloat16 [32, 4, 8, 128, 128], P('row', 'col', 'depth')
Inputs may be any that keep to these rules, and one draw needn't show every extreme that they name: `a_columns`: columns of one block row and group g are distinct and lie in g * 10 to (g + 1) * 10 - 1, also in empty slots. `atom_rows`: A permutation that maps every aligned run of 8 atom-order rows onto the same run of block rows. `b_columns`: columns of one block row and panel c are distinct and lie in c * 80 to (c + 1) * 80 - 1, also in empty slots. `b_live`: live slots of block row k hold columns within 16 of k, counted round. `c_columns`: columns of one block row and panel c are distinct and lie in c * 80 to (c + 1) * 80 - 1.
All inputs are finite; a program needn't handle non-finite values.
Results may differ from a plain program's by a relative error of at most 0.0043.
Values may be sent and summed in bfloat16 or wider, within the bound.
A program may use at most 320 MiB of HBM per device.

v0:
```python
import jax
import jax.numpy as jnp
from jax import lax
from jax.sharding import PartitionSpec as P

GW = 10


def shifted(value, axis, by):
    length = lax.axis_size(axis)
    return lax.ppermute(value, axis, [(i, (i + by) % length) for i in range(length)])


def on_device(
    a_blocks, a_columns, a_live, atom_rows, b_blocks, b_columns, b_live, c_columns, c_live
):
    row_count = lax.axis_size("row")
    col_count = lax.axis_size("col")
    depth_count = lax.axis_size("depth")
    turn_count = min(row_count, col_count)
    row_index = lax.axis_index("row")
    own_rows, group_count, slot_count = a_columns.shape
    block_edge = a_blocks.shape[-1]
    stripe = b_blocks.shape[0]
    per_stripe = stripe // GW
    stripes_piece = row_count // turn_count
    piece_groups = stripes_piece * per_stripe
    dest_col = jnp.arange(col_count, dtype=jnp.int32)[:, None, None]
    dest_layer = jnp.arange(depth_count, dtype=jnp.int32)[None, :, None]
    within = jnp.arange(piece_groups, dtype=jnp.int32)[None, None, :]
    piece_of = (dest_col + row_index) % turn_count
    stripe_ids = (piece_of * stripes_piece + within // per_stripe) * depth_count + dest_layer
    group_ids = (stripe_ids * per_stripe + within % per_stripe).reshape(-1)
    lead_shape = (col_count, depth_count, own_rows, piece_groups, slot_count)
    send_blocks = jnp.moveaxis(jnp.take(a_blocks, group_ids, axis=1), 1, 0).reshape(
        lead_shape + (block_edge, block_edge)
    )
    send_columns = jnp.moveaxis(jnp.take(a_columns, group_ids, axis=1), 1, 0).reshape(lead_shape)
    outgoing_live_flags = jnp.moveaxis(jnp.take(a_live, group_ids, axis=1), 1, 0).reshape(
        lead_shape
    )
    send_rows = jnp.broadcast_to(atom_rows[None, None, :], (col_count, depth_count, own_rows))
    pair_count = col_count * depth_count
    got_blocks, got_columns, got_live, got_rows = (
        lax.all_to_all(
            send_blocks.reshape((pair_count,) + lead_shape[2:] + (block_edge, block_edge)),
            ("col", "depth"),
            split_axis=0,
            concat_axis=0,
            tiled=True,
        ),
        lax.all_to_all(
            send_columns.reshape((pair_count,) + lead_shape[2:]),
            ("col", "depth"),
            split_axis=0,
            concat_axis=0,
            tiled=True,
        ),
        lax.all_to_all(
            outgoing_live_flags.reshape((pair_count,) + lead_shape[2:]),
            ("col", "depth"),
            split_axis=0,
            concat_axis=0,
            tiled=True,
        ),
        lax.all_to_all(
            send_rows.reshape(pair_count, own_rows),
            ("col", "depth"),
            split_axis=0,
            concat_axis=0,
            tiled=True,
        ),
    )
    panel_rows = got_rows.reshape(-1)
    panel_count = panel_rows.shape[0]
    local_rows = panel_rows - row_index * panel_count
    positions = jnp.arange(panel_count, dtype=jnp.int32)
    matched_pairs = local_rows[None, :] == positions[:, None]
    source_of = jnp.sum(jnp.where(matched_pairs, positions[None, :], 0), axis=1)
    block_tiles = got_blocks.reshape(panel_count, -1, block_edge, block_edge)
    columns = got_columns.reshape(panel_count, -1)
    live_flags = got_live.reshape(panel_count, -1)
    layer_blocks, layer_columns, layer_active_flags = (
        lax.all_gather(b_blocks, "row", axis=0, tiled=True),
        lax.all_gather(b_columns, "row", axis=0, tiled=True),
        lax.all_gather(b_live, "row", axis=0, tiled=True),
    )
    list_width = b_columns.shape[2]
    layer_blocks = layer_blocks.reshape(-1, list_width, block_edge, block_edge)
    layer_columns = layer_columns.reshape(-1, list_width)
    layer_active_flags = layer_active_flags.reshape(-1, list_width)
    wanted = jnp.take(c_columns[:, 0, :], local_rows, axis=0)
    partial_value = jnp.zeros((panel_count, wanted.shape[1], block_edge, block_edge), jnp.float32)
    for turn_index in range(turn_count):
        layer_row_index = columns // stripe // depth_count * stripe + columns % stripe
        found_columns = jnp.take(layer_columns, layer_row_index, axis=0)
        found_live = jnp.take(layer_active_flags, layer_row_index, axis=0)
        usable = (found_live > 0) & (live_flags[:, :, None] > 0)
        hits = (found_columns[:, None, :, :] == wanted[:, :, None, None]) & usable[:, None, :, :]
        mapping = hits.astype(jnp.float32)
        selected_entries = jnp.take(layer_blocks, layer_row_index, axis=0)
        block_products = jnp.einsum(
            "rvab,rvsbe->rvsae", block_tiles, selected_entries, preferred_element_type=jnp.float32
        )
        partial_value = partial_value + jnp.einsum(
            "ruvs,rvsae->ruae", mapping, block_products, precision=lax.Precision.HIGHEST
        )
        if turn_index + 1 < turn_count:
            block_tiles, columns, live_flags = shifted(
                (block_tiles, columns, live_flags), "col", -1
            )
    share_count = wanted.shape[1] // depth_count
    depth_index = lax.axis_index("depth")
    summed = lax.psum(partial_value.astype(jnp.bfloat16), "depth").astype(jnp.float32)
    my_share = lax.dynamic_slice_in_dim(summed, depth_index * share_count, share_count, 1)
    my_share = jnp.take(my_share, source_of, axis=0)
    keep_flags = lax.dynamic_slice_in_dim(
        c_live[:, 0, :], depth_index * share_count, share_count, 1
    )
    result = jnp.where(keep_flags[..., None, None] > 0, my_share, jnp.float32(0.0)).astype(
        jnp.bfloat16
    )
    return result[:, None]


def solution(mesh):
    placed = (
        P(("row", "col", "depth"), None, None, None, None),
        P(("row", "col", "depth"), None, None),
        P(("row", "col", "depth"), None, None),
        P(("row", "col", "depth")),
        P(("row", "depth"), "col", None, None, None),
        P(("row", "depth"), "col", None),
        P(("row", "depth"), "col", None),
        P("row", "col", None),
        P("row", "col", None),
    )
    return jax.shard_map(
        on_device,
        mesh=mesh,
        in_specs=placed,
        out_specs=P("row", "col", "depth", None, None),
        check_vma=False,
    )
```

profile of v0, /device:TPU:0, one launch (start us, length us, event | category | flops | bytes accessed | tf_op | source)
XLA Modules:
  0.0 684.4 jit_solution(8725497915445718610)
XLA Ops:
  48.0 27.6 %all-to-all-done.3 = bf16[8,1,4,2,128,128]{5,4,3,2,1,0:T(8,128)(2,1)} async-done(((bf16[8,1,4,2,128,128]{5,4,3,2,1,0:T(8,128)(2,1)}), bf16[8,1,4,2,128,128]{5,4,3,2,1,0:T(8,128)(2,1)}, u32[]{:S(2)}, u32[]{:S(2)}) %all-to-all-start.3) | async-done | bytes 2097184 | tf_op jit(solution)/shard_map/all_to_all | solution.py:45
  92.0 37.3 %all-to-all-done.2 = s32[8,1,4,2]{2,3,1,0:T(2,128)S(1)} async-done(((s32[8,1,4,2]{2,3,1,0:T(2,128)}), s32[8,1,4,2]{2,3,1,0:T(2,128)S(1)}, u32[]{:S(2)}, u32[]{:S(2)}) %all-to-all-start.2) | async-done | bytes 288 | tf_op jit(solution)/shard_map/all_to_all | solution.py:59
  142.2 42.9 %collective-permute-done.4 = s32[8,8]{0,1:T(8,128)S(1)} collective-permute-done((s32[8,8]{0,1:T(8,128)S(1)}, s32[8,8]{0,1:T(8,128)S(1)}, u32[]{:S(2)}, u32[]{:S(2)}) %collective-permute-start.4) | collective-permute-done | bytes 288 | tf_op jit(solution)/shard_map/ppermute | solution.py:11
  197.2 95.8 %all-gather.2.cloned.1.call-done = bf16[160,1,6,128,128]{4,3,2,1,0:T(8,128)(2,1)} async-done(((bf16[40,1,6,128,128]{4,3,2,1,0:T(8,128)(2,1)}), bf16[160,1,6,128,128]{4,3,2,1,0:T(8,128)(2,1)}) %all-gather.2.cloned.1.call-update) | async-done | bytes 31457296 | tf_op jit(solution)/shard_map/all_gather | solution.py:84
  293.0 17.2 %gather_fusion.7 = bf16[64,6,128,128]{3,2,1,0:T(8,128)(2,1)} fusion(bf16[160,6,128,128]{3,2,1,0:T(8,128)(2,1)} %bitcast.147, s32[1024]{0:T(1024)S(1)} %pad_clamp_fusion.6), kind=kCustom, calls=%fused_computation.2.clone | custom fusion | bytes 25166080 | tf_op jit(solution)/shard_map/jit(_take)/gather | solution.py:101
  310.3 17.2 %gather_fusion.10 = bf16[64,6,128,128]{3,2,1,0:T(8,128)(2,1)} fusion(bf16[160,6,128,128]{3,2,1,0:T(8,128)(2,1)} %bitcast.148, s32[1024]{0:T(1024)S(1)} %pad_clamp_fusion.3), kind=kCustom, calls=%fused_computation.11.clone | custom fusion | bytes 25166080 | tf_op jit(solution)/shard_map/jit(_take)/gather | solution.py:101
  327.5 16.6 %copy.239 = bf16[8,8,6,128,128]{3,4,2,1,0:T(8,128)(2,1)} copy(bf16[8,8,6,128,128]{4,3,2,1,0:T(8,128)(2,1)} %bitcast.153) | data formatting | bytes 25165824 | tf_op jit(solution)/shard_map/jit(_take)/gather | solution.py:101
  344.1 16.7 %copy.250 = bf16[8,8,6,128,128]{3,4,2,1,0:T(8,128)(2,1)} copy(bf16[8,8,6,128,128]{4,3,2,1,0:T(8,128)(2,1)} %bitcast.154) | data formatting | bytes 25165824 | tf_op jit(solution)/shard_map/jit(_take)/gather | solution.py:101
  360.8 13.6 %fusion.12 = f32[8,8,6,128,128]{3,4,2,1,0:T(8,128)} fusion(bf16[8,8,128,128,1]{3,2,4,1,0:T(8,128)(2,1)} %bitcast.24, bf16[8,8,6,128,128]{3,4,2,1,0:T(8,128)(2,1)} %copy.239, pred[8,8]{1,0:T(8,128)(4,1)S(1)} %copy.224), kind=kOutput, calls=%fused_computation.29 | convolution fusion | flops 1616904192 | bytes 39845952 | tf_op jit(solution)/shard_map/rvab,rvsbe->rvsae/dot_general | solution.py:102
  374.4 13.7 %fusion.15 = f32[8,8,6,128,128]{3,4,2,1,0:T(8,128)} fusion(bf16[8,8,6,128,128]{3,4,2,1,0:T(8,128)(2,1)} %copy.250, pred[8,8]{1,0:T(8,128)(4,1)S(1)} %copy.241, bf16[8,8,128,128]{3,2,1,0:T(8,128)(2,1)} %collective-permute-done.2), kind=kOutput, calls=%fused_computation.30 | convolution fusion | flops 1616904192 | bytes 39845952 | tf_op jit(solution)/shard_map/rvab,rvsbe->rvsae/dot_general | solution.py:102
  388.1 17.3 %gather_fusion.13 = bf16[64,6,128,128]{3,2,1,0:T(8,128)(2,1)} fusion(bf16[160,6,128,128]{3,2,1,0:T(8,128)(2,1)} %bitcast.149, s32[1024]{0:T(1024)S(1)} %pad_clamp_fusion.2), kind=kCustom, calls=%fused_computation.12.clone | custom fusion | bytes 25166080 | tf_op jit(solution)/shard_map/jit(_take)/gather | solution.py:101
  405.4 17.2 %gather_fusion.16 = bf16[64,6,128,128]{3,2,1,0:T(8,128)(2,1)} fusion(bf16[160,6,128,128]{3,2,1,0:T(8,128)(2,1)} %bitcast.150, s32[1024]{0:T(1024)S(1)} %pad_clamp_fusion.1), kind=kCustom, calls=%fused_computation.13.clone | custom fusion | bytes 25166080 | tf_op jit(solution)/shard_map/jit(_take)/gather | solution.py:101
  422.5 24.8 %copy.240 = f32[8,8,6,128,128]{4,1,2,3,0:T(8,128)} copy(f32[8,8,6,128,128]{3,4,2,1,0:T(8,128)} %fusion.12) | data formatting | bytes 50331648 | tf_op jit(solution)/shard_map/rvab,rvsbe->rvsae/transpose | solution.py:102
  447.3 24.9 %copy.251 = f32[8,8,6,128,128]{4,1,2,3,0:T(8,128)} copy(f32[8,8,6,128,128]{3,4,2,1,0:T(8,128)} %fusion.15) | data formatting | bytes 50331648 | tf_op jit(solution)/shard_map/rvab,rvsbe->rvsae/transpose | solution.py:102
  472.2 16.6 %copy.272 = bf16[8,8,6,128,128]{3,4,2,1,0:T(8,128)(2,1)} copy(bf16[8,8,6,128,128]{4,3,2,1,0:T(8,128)(2,1)} %bitcast.152) | data formatting | bytes 25165824 | tf_op jit(solution)/shard_map/jit(_take)/gather | solution.py:101
  488.8 16.7 %copy.261 = bf16[8,8,6,128,128]{3,4,2,1,0:T(8,128)(2,1)} copy(bf16[8,8,6,128,128]{4,3,2,1,0:T(8,128)(2,1)} %bitcast.151) | data formatting | bytes 25165824 | tf_op jit(solution)/shard_map/jit(_take)/gather | solution.py:101
  505.5 13.8 %fusion.18 = f32[8,8,6,128,128]{3,4,2,1,0:T(8,128)} fusion(bf16[8,8,6,128,128]{3,4,2,1,0:T(8,128)(2,1)} %copy.261, pred[8,8]{1,0:T(8,128)(4,1)S(1)} %copy.252, bf16[8,8,128,128]{3,2,1,0:T(8,128)(2,1)} %collective-permute-done.5), kind=kOutput, calls=%fused_computation.31 | convolution fusion | flops 1616904192 | bytes 39845952 | tf_op jit(solution)/shard_map/rvab,rvsbe->rvsae/dot_general | solution.py:102
  519.2 24.8 %copy.262 = f32[8,8,6,128,128]{4,1,2,3,0:T(8,128)} copy(f32[8,8,6,128,128]{3,4,2,1,0:T(8,128)} %fusion.18) | data formatting | bytes 50331648 | tf_op jit(solution)/shard_map/rvab,rvsbe->rvsae/transpose | solution.py:102
  556.9 24.9 %copy.273 = f32[8,8,6,128,128]{4,1,2,3,0:T(8,128)} copy(f32[8,8,6,128,128]{3,4,2,1,0:T(8,128)} %fusion.21) | data formatting | bytes 50331648 | tf_op jit(solution)/shard_map/rvab,rvsbe->rvsae/transpose | solution.py:102
  581.9 15.6 %fusion.39 = f32[8,8,128,128,1]{3,1,4,2,0:T(8,128)} fusion(f32[8,8,6,128,128]{4,1,2,3,0:T(8,128)} %copy.240, s32[8,8]{1,0:T(8,128)S(1)} %copy-done.7, s32[8,8,6]{1,2,0:T(8,128)S(1)} %copy-done.3, pred[8,8,6]{1,2,0:T(8,128)(4,1)S(1)} %copy-done.8), kind=kOutput, calls=%fused_computation.54 | convolution fusion | flops 603985920 | bytes 29362304 | tf_op jit(solution)/shard_map/ruvs,rvsae->ruae/dot_general | solution.py:105
  597.5 15.6 %fusion.37 = f32[8,8,128,128,1]{3,1,4,2,0:T(8,128)} fusion(f32[8,8,6,128,128]{4,1,2,3,0:T(8,128)} %copy.251, s32[8,8,6]{1,2,0:T(8,128)S(1)} %copy-done.4, s32[8,8]{1,0:T(8,128)S(1)} %copy-done.7, pred[8,8,6]{1,2,0:T(8,128)(4,1)S(1)} %copy-done.9), kind=kOutput, calls=%fused_computation.52 | convolution fusion | flops 603985920 | bytes 29362304 | tf_op jit(solution)/shard_map/ruvs,rvsae->ruae/dot_general | solution.py:105
  613.1 15.9 %fusion.35 = f32[8,8,128,128,1]{3,1,4,2,0:T(8,128)} fusion(f32[8,8,6,128,128]{4,1,2,3,0:T(8,128)} %copy.262, s32[8,8,6]{1,2,0:T(8,128)S(1)} %copy-done.5, s32[8,8]{1,0:T(8,128)S(1)} %copy-done.7, pred[8,8,6]{1,2,0:T(8,128)(4,1)S(1)} %copy-done.10), kind=kOutput, calls=%fused_computation.50 | convolution fusion | flops 603985920 | bytes 29362304 | tf_op jit(solution)/shard_map/ruvs,rvsae->ruae/dot_general | solution.py:105
  629.0 19.4 %fusion.28 = bf16[8,8,128,128]{3,1,2,0:T(8,128)(2,1)} fusion(f32[8,8,128,128,1]{3,1,4,2,0:T(8,128)} %fusion.35, f32[8,8,128,128,1]{3,1,4,2,0:T(8,128)} %fusion.37, f32[8,8,128,128,1]{3,1,4,2,0:T(8,128)} %fusion.39, f32[8,8,6,128,128]{4,1,2,3,0:T(8,128)} %copy.273, s32[8,8,6]{1,2,0:T(8,128)S(1)} %copy-done.6, s32[8,8]{1,0:T(8,128)S(1)} %copy-done.7, ...), kind=kOutput, calls=%fused_computation.38 | convolution fusion | flops 608180224 | bytes 39848064 | tf_op jit(solution)/shard_map/ruvs,rvsae->ruae/dot_general | solution.py:105
  648.8 20.9 %all-reduce.2.cloned.1.call-done = bf16[8,8,128,128]{3,1,2,0:T(8,128)(2,1)} async-done(((bf16[8,8,128,128]{3,1,2,0:T(8,128)(2,1)}), bf16[8,8,128,128]{3,1,2,0:T(8,128)(2,1)}) %all-reduce.2.cloned.1.call-update) | async-done | bytes 2097168 | tf_op jit(solution)/shard_map/psum | solution.py:114
  (168 shorter events, 102.9 us)
Async XLA Ops:
  6.5 20.7 %copy-start.16 = (s32[1,32,2]{1,2,0:T(2,128)S(1)}, s32[1,32,2]{1,2,0:T(2,128)}, u32[]{:S(2)}) copy-start(s32[1,32,2]{1,2,0:T(2,128)} %param.17) | copy-start | bytes 772
  6.5 22.9 %copy-start.13 = (s32[40,1,6]{0,1,2:T(1,128)S(1)}, s32[40,1,6]{0,1,2:T(1,128)}, u32[]{:S(2)}) copy-start(s32[40,1,6]{0,1,2:T(1,128)} %param.20) | copy-start | bytes 2884
  6.5 22.9 %copy-start.14 = (s32[40,1,6]{0,1,2:T(1,128)S(1)}, s32[40,1,6]{0,1,2:T(1,128)}, u32[]{:S(2)}) copy-start(s32[40,1,6]{0,1,2:T(1,128)} %param.21) | copy-start | bytes 2884
  6.5 76.1 %copy-start.2 = (s32[8,1,8]{2,1,0:T(1,128)S(1)}, s32[8,1,8]{2,1,0:T(1,128)}, u32[]{:S(2)}) copy-start(s32[8,1,8]{2,1,0:T(1,128)} %param.22) | copy-start | bytes 772
  6.6 286.5 %all-gather.2.cloned.1.call-start = ((), (), s32[]{:S(2)}) async-start(), calls=%async_computation.4 | async-start | bytes 39321600 | tf_op jit(solution)/shard_map/all_gather | solution.py:84
  8.5 12.7 %all-to-all-start = ((s32[8,1,1]{2,1,0:T(1,128)}), s32[8,1,1]{2,1,0:T(1,128)S(1)}, u32[]{:S(2)}, u32[]{:S(2)}) async-start(s32[8,1,1]{2,1,0:T(1,128)} %reshape.365), calls=%async_computation | async-start | bytes 8192 | tf_op jit(solution)/shard_map/all_to_all | solution.py:66
  21.2 54.4 %all-to-all-start.3 = ((bf16[8,1,4,2,128,128]{5,4,3,2,1,0:T(8,128)(2,1)}), bf16[8,1,4,2,128,128]{5,4,3,2,1,0:T(8,128)(2,1)}, u32[]{:S(2)}, u32[]{:S(2)}) async-start(bf16[8,1,4,2,128,128]{5,4,3,2,1,0:T(8,128)(2,1)} %broadcast_select_fusion), calls=%async_computation.3 | async-start | bytes 4194304 | tf_op jit(solution)/shard_map/all_to_all | solution.py:45
  47.9 36.6 %copy-start.17 = (s32[8]{0:T(128)}, s32[8]{0:T(128)S(1)}, u32[]{:S(2)}) copy-start(s32[8]{0:T(128)S(1)} %subtract_reduce_fusion) | copy-start | bytes 100
  75.6 8.9 %all-to-all-start.1 = ((s32[8,1,4,2]{2,3,1,0:T(2,128)}), s32[8,1,4,2]{2,3,1,0:T(2,128)S(1)}, u32[]{:S(2)}, u32[]{:S(2)}) async-start(s32[8,1,4,2]{2,3,1,0:T(2,128)} %copy.222), calls=%async_computation.1 | async-start | bytes 16384 | tf_op jit(solution)/shard_map/all_to_all | solution.py:52
  78.9 59.5 %collective-permute-start.2 = (bf16[8,8,128,128]{3,2,1,0:T(8,128)(2,1)}, bf16[8,8,128,128]{3,2,1,0:T(8,128)(2,1)}, u32[]{:S(2)}, u32[]{:S(2)}) collective-permute-start(bf16[8,8,128,128]{3,2,1,0:T(8,128)(2,1)} %bitcast.22), channel_id=1, source_target_pairs={{0,6},{2,0},{4,2},{6,4},{1,7},{3,1},{5,3},{7,5},{8,14},{10,8},{12,... | collective-permute-start | bytes 6291464 | tf_op jit(solution)/shard_map/ppermute | solution.py:11
  84.5 44.8 %all-to-all-start.2 = ((s32[8,1,4,2]{2,3,1,0:T(2,128)}), s32[8,1,4,2]{2,3,1,0:T(2,128)S(1)}, u32[]{:S(2)}, u32[]{:S(2)}) async-start(s32[8,1,4,2]{2,3,1,0:T(2,128)} %copy.233), calls=%async_computation.2 | async-start | bytes 16384 | tf_op jit(solution)/shard_map/all_to_all | solution.py:59
  87.8 582.0 %all-reduce.2.cloned.1.call-start = ((), (), s32[]{:S(2)}) async-start(), calls=%async_computation.5 | async-start | bytes 4194304 | tf_op jit(solution)/shard_map/psum | solution.py:114
  88.0 47.7 %collective-permute-start = (s32[8,8]{0,1:T(8,128)S(1)}, s32[8,8]{0,1:T(8,128)S(1)}, u32[]{:S(2)}, u32[]{:S(2)}) collective-permute-start(s32[8,8]{0,1:T(8,128)S(1)} %bitcast.168), channel_id=1, source_target_pairs={{0,6},{2,0},{4,2},{6,4},{1,7},{3,1},{5,3},{7,5},{8,14},{10,8},{12,... | collective-permute-start | bytes 776 | tf_op jit(solution)/shard_map/ppermute | solution.py:11
  129.4 7.6 %collective-permute-start.1 = (s32[8,8]{0,1:T(8,128)S(1)}, s32[8,8]{0,1:T(8,128)S(1)}, u32[]{:S(2)}, u32[]{:S(2)}) collective-permute-start(s32[8,8]{0,1:T(8,128)S(1)} %bitcast.165), channel_id=1, source_target_pairs={{0,6},{2,0},{4,2},{6,4},{1,7},{3,1},{5,3},{7,5},{8,14},{10,8},{12,... | collective-permute-start | bytes 776 | tf_op jit(solution)/shard_map/ppermute | solution.py:11
  137.2 3.6 collective-permute-start.3
  138.4 56.6 %collective-permute-start.5 = (bf16[8,8,128,128]{3,2,1,0:T(8,128)(2,1)}, bf16[8,8,128,128]{3,2,1,0:T(8,128)(2,1)}, u32[]{:S(2)}, u32[]{:S(2)}) collective-permute-start(bf16[8,8,128,128]{3,2,1,0:T(8,128)(2,1)} %collective-permute-done.2), channel_id=1, source_target_pairs={{0,6},{2,0},{4,2},{6,4},{1,7},{3,1},{5,3},{7,5},{8,14},{10,8},{12,... | collective-permute-start | bytes 6291464 | tf_op jit(solution)/shard_map/ppermute | solution.py:11
  140.0 45.1 %collective-permute-start.4 = (s32[8,8]{0,1:T(8,128)S(1)}, s32[8,8]{0,1:T(8,128)S(1)}, u32[]{:S(2)}, u32[]{:S(2)}) collective-permute-start(s32[8,8]{0,1:T(8,128)S(1)} %collective-permute-done.1), channel_id=1, source_target_pairs={{0,6},{2,0},{4,2},{6,4},{1,7},{3,1},{5,3},{7,5},{8,14},{10,8},{12,... | collective-permute-start | bytes 776 | tf_op jit(solution)/shard_map/ppermute | solution.py:11
  185.3 4.3 collective-permute-start.6
  189.6 3.6 collective-permute-start.7
  195.0 349.1 %collective-permute-start.8 = (bf16[8,8,128,128]{3,2,1,0:T(8,128)(2,1)}, bf16[8,8,128,128]{3,2,1,0:T(8,128)(2,1)S(1)}, u32[]{:S(2)}, u32[]{:S(2)}) collective-permute-start(bf16[8,8,128,128]{3,2,1,0:T(8,128)(2,1)} %collective-permute-done.5), channel_id=1, source_target_pairs={{0,6},{2,0},{4,2},{6,4},{1,7},{3,1},{5,3},{7,5},{8,14},{10,8},{12,... | collective-permute-start | bytes 6291464 | tf_op jit(solution)/shard_map/ppermute | solution.py:11
  556.9 24.9 %copy-start.3 = (s32[8,8,6]{1,2,0:T(8,128)S(1)}, s32[8,8,6]{1,2,0:T(8,128)}, u32[]{:S(2)}) copy-start(s32[8,8,6]{1,2,0:T(8,128)} %copy.227) | copy-start | bytes 4612
  556.9 24.9 %copy-start.7 = (s32[8,8]{1,0:T(8,128)S(1)}, s32[8,8]{1,0:T(8,128)}, u32[]{:S(2)}) copy-start(s32[8,8]{1,0:T(8,128)} %broadcast_select_fusion.1) | copy-start | bytes 772
  556.9 24.9 %copy-start.8 = (pred[8,8,6]{1,2,0:T(8,128)(4,1)S(1)}, pred[8,8,6]{1,2,0:T(8,128)(4,1)}, u32[]{:S(2)}) copy-start(pred[8,8,6]{1,2,0:T(8,128)(4,1)} %copy.236) | copy-start | bytes 1156
  629.0 48.3 %copy-start.1 = (bf16[1,32,2,128,128]{4,3,2,1,0:T(8,128)(2,1)S(1)}, bf16[1,32,2,128,128]{4,3,2,1,0:T(8,128)(2,1)}, u32[]{:S(2)}) copy-start(bf16[1,32,2,128,128]{4,3,2,1,0:T(8,128)(2,1)} %param.15) | copy-start | bytes 6291460
  (10 other events, 161.9 us)
Sparse Core Ops, SparseCore 0:
  9.3 283.7 all-gather.1
  648.6 21.1 all-reduce.1
where the time goes:
time: 692 us; the launch traced here: 684 us
  local copies, waits for them, and re-layouts  259 us (37%)
  waiting for transfers between devices  228 us (33%)
  matrix products  120 us (17%)
  starting transfers between devices  35.6 us (5%)
  blocking collectives  18.1 us (3%)
  between operations  14.6 us (2%)
  other arithmetic  7.82 us (1%)
    gather x8, local copies, waits for them, and re-layouts, on_device(): selected_entries = jnp.take(layer_blocks, layer_row_index, axis=0)  135 us
    transpose x4, local copies, waits for them, and re-layouts, on_device(): jnp.einsum('rvab,rvsbe->rvsae', block_tiles, selected_entries, preferred_...  99.4 us
    all_gather x1, waiting for transfers between devices, on_device(): lax.all_gather(b_blocks, 'row', axis=0, tiled=True)  95.8 us
    dot_general x4, matrix products, on_device(): jnp.einsum('ruvs,rvsae->ruae', mapping, block_products, precision=lax.Pre...  66.5 us
    dot_general x4, matrix products, on_device(): jnp.einsum('rvab,rvsbe->rvsae', block_tiles, selected_entries, preferred_...  53.9 us
    ppermute x9, waiting for transfers between devices, shifted(): lax.ppermute(value, axis, [(i, (i + by) % length) for i in range(length)])  45.5 us
    all_to_all x1, waiting for transfers between devices, on_device(): lax.all_to_all(outgoing_live_flags.reshape((pair_count,) + lead_shape[2:]...  37.3 us
    all_to_all x1, waiting for transfers between devices, on_device(): lax.all_to_all(send_blocks.reshape((pair_count,) + lead_shape[2:] + (bloc...  27.6 us
  transfers between devices with their start and end apart: 15, of which 8 were waited for; matrix products, arithmetic and copies ran while one was open for 40% of the time, Pallas kernels for 0%

commit v1 on v0

--- a/solution.py
+++ b/solution.py
@@ -4,6 +4,18 @@
 from jax.sharding import PartitionSpec as P
 
 GW = 10
+
+
+def collect(value, axis, dim):
+    ways, here, step = (lax.axis_size(axis), lax.axis_index(axis), value.shape[dim])
+    line, have = (value, 1)
+    while have < ways:
+        line = jnp.concatenate(
+            [line, lax.ppermute(line, axis, [(d, (d - have) % ways) for d in range(ways)])],
+            axis=dim,
+        )
+        have = 2 * have
+    return jnp.roll(line, here * step, axis=dim)
 
 
 def shifted(value, axis, by):
@@ -81,7 +93,7 @@
     columns = got_columns.reshape(panel_count, -1)
     live_flags = got_live.reshape(panel_count, -1)
     layer_blocks, layer_columns, layer_active_flags = (
-        lax.all_gather(b_blocks, "row", axis=0, tiled=True),
+        collect(b_blocks, "row", 0),
         lax.all_gather(b_columns, "row", axis=0, tiled=True),
         lax.all_gather(b_live, "row", axis=0, tiled=True),
     )

time: 692 us -> 1150 us (1.66)
  blocking collectives: 18.1 us -> 330 us
  local copies, waits for them, and re-layouts: 259 us -> 347 us
  waiting for transfers between devices: 228 us -> 270 us
    all_gather x1, blocking collectives: 9.06 us -> 322 us  [on_device(): lax.all_gather(b_columns, 'row', axis=0, tiled=True)]
    ppermute x0 -> x2, waiting for transfers between devices: none -> 169 us  [collect(): lax.ppermute(line, axis, [(d, (d - have) % ways) for d in range(ways)])]
    all_gather x1 -> x0, waiting for transfers between devices: 95.8 us -> none  [on_device(): lax.all_gather(b_blocks, 'row', axis=0, tiled=True)]
    unnamed x41 -> x52, local copies, waits for them, and re-layouts: 0.34 us -> 53.7 us
    all_to_all x1, waiting for transfers between devices: 27.6 us -> 0.01 us  [on_device(): lax.all_to_all(send_blocks.reshape((pair_count,) + lead_shape[2:] + (bloc...]
    reshape x0 -> x1, local copies, waits for them, and re-layouts: none -> 21.8 us  [on_device(): layer_blocks = layer_blocks.reshape(-1, list_width, block_edge, block_edge)]
    concatenate x0 -> x1, local copies, waits for them, and re-layouts: none -> 13.5 us  [collect(): return jnp.roll(line, here * step, axis=dim)]
    concatenate x0 -> x1, other arithmetic: none -> 11.9 us  [collect(): jnp.concatenate([line, lax.ppermute(line, axis, [(d, (d - have) % ways) f...]
  transfers between devices with their start and end apart: 15 -> 16, of which waited for: 8 -> 7; matrix products, arithmetic and copies ran while one was open for 40% -> 32% of each run, Pallas kernels for 0% -> 0%
where the time goes in v1:
time: 1150 us; the launch traced here: 1140 us
  local copies, waits for them, and re-layouts  347 us (30%)
  blocking collectives  330 us (29%)
  waiting for transfers between devices  270 us (23%)
  matrix products  121 us (11%)
  starting transfers between devices  40.9 us (4%)
  other arithmetic  18.9 us (2%)
  between operations  14.5 us (1%)
    all_gather x1, blocking collectives, on_device(): lax.all_gather(b_columns, 'row', axis=0, tiled=True)  322 us
    ppermute x2, waiting for transfers between devices, collect(): lax.ppermute(line, axis, [(d, (d - have) % ways) for d in range(ways)])  169 us
    gather x8, local copies, waits for them, and re-layouts, on_device(): selected_entries = jnp.take(layer_blocks, layer_row_index, axis=0)  135 us
    transpose x4, local copies, waits for them, and re-layouts, on_device(): jnp.einsum('rvab,rvsbe->rvsae', block_tiles, selected_entries, preferred_...  99.2 us
    dot_general x4, matrix products, on_device(): jnp.einsum('ruvs,rvsae->ruae', mapping, block_products, precision=lax.Pre...  66.8 us
    dot_general x4, matrix products, on_device(): jnp.einsum('rvab,rvsbe->rvsae', block_tiles, selected_entries, preferred_...  54.6 us
    unnamed x52, local copies, waits for them, and re-layouts  53.7 us
    ppermute x9, waiting for transfers between devices, shifted(): lax.ppermute(value, axis, [(i, (i + by) % length) for i in range(length)])  44.4 us
  transfers between devices with their start and end apart: 16, of which 7 were waited for; matrix products, arithmetic and copies ran while one was open for 32% of the time, Pallas kernels for 0%

profile of v1, /device:TPU:0, one launch (start us, length us, event | category | flops | bytes accessed | tf_op | source)
XLA Modules:
  0.0 1143.0 jit_solution(3638023576839842180)
XLA Ops:
  10.4 168.8 %collective-permute-done = bf16[40,1,6,128,128]{4,3,2,1,0:T(8,128)(2,1)S(1)} collective-permute-done((bf16[40,1,6,128,128]{4,3,2,1,0:T(8,128)(2,1)}, bf16[40,1,6,128,128]{4,3,2,1,0:T(8,128)(2,1)S(1)}, u32[]{:S(2)}, u32[]{:S(2)}) %collective-permute-start) | collective-permute-done | bytes 7864352 | tf_op jit(solution)/shard_map/ppermute | solution.py:14
  212.6 321.8 %all_gather.6 = s32[160,1,6]{2,0,1:T(8,128)S(1)} all-gather(s32[40,1,6]{2,0,1:T(8,128)S(1)} %copy.221), channel_id=1, replica_groups=mesh['row'=4,'col'=4,'depth'=2] {'row'}, dimensions={0}, use_global_device_ids=true | all-gather | bytes 4800 | tf_op jit(solution)/shard_map/all_gather | solution.py:97
  571.9 37.0 %all-to-all-done.2 = s32[8,1,4,2]{2,3,1,0:T(2,128)S(1)} async-done(((s32[8,1,4,2]{2,3,1,0:T(2,128)}), s32[8,1,4,2]{2,3,1,0:T(2,128)S(1)}, u32[]{:S(2)}, u32[]{:S(2)}) %all-to-all-start.2) | async-done | bytes 288 | tf_op jit(solution)/shard_map/all_to_all | solution.py:71
  622.1 42.8 %collective-permute-done.6 = s32[8,8]{0,1:T(8,128)S(1)} collective-permute-done((s32[8,8]{0,1:T(8,128)S(1)}, s32[8,8]{0,1:T(8,128)S(1)}, u32[]{:S(2)}, u32[]{:S(2)}) %collective-permute-start.6) | collective-permute-done | bytes 288 | tf_op jit(solution)/shard_map/ppermute | solution.py:23
  685.6 13.7 %constant_dynamic-update-slice_fusion.3 = bf16[320,1,6,128,128]{4,3,2,1,0:T(8,128)(2,1)} fusion(bf16[320,1,6,128,128]{4,3,2,1,0:T(8,128)(2,1)} %constant_dynamic-update-slice_fusion.4, bf16[80,1,6,128,128]{4,3,2,1,0:T(8,128)(2,1)} %collective-permute-done.1), kind=kLoop, calls=%fused_computation.97 | loop fusion | bytes 31457280
  732.5 21.8 %dynamic-slice_bitcast_fusion = bf16[160,6,128,128]{3,2,1,0:T(8,128)(2,1)} fusion(bf16[320,1,6,128,128]{4,3,2,1,0:T(8,128)(2,1)} %constant_dynamic-update-slice_fusion, s32[]{:T(128)S(6)} %select_n.229), kind=kLoop, calls=%fused_computation.17 | loop fusion | bytes 62914564 | tf_op jit(solution)/shard_map/reshape | solution.py:101
  754.3 17.2 %gather_fusion.13 = bf16[64,6,128,128]{3,2,1,0:T(8,128)(2,1)} fusion(bf16[160,6,128,128]{3,2,1,0:T(8,128)(2,1)} %dynamic-slice_bitcast_fusion, s32[1024]{0:T(1024)S(1)} %pad_clamp_fusion.2), kind=kCustom, calls=%fused_computation.12.clone | custom fusion | bytes 25166080 | tf_op jit(solution)/shard_map/jit(_take)/gather | solution.py:113
  771.5 17.2 %gather_fusion.10 = bf16[64,6,128,128]{3,2,1,0:T(8,128)(2,1)} fusion(bf16[160,6,128,128]{3,2,1,0:T(8,128)(2,1)} %dynamic-slice_bitcast_fusion, s32[1024]{0:T(1024)S(1)} %pad_clamp_fusion.3), kind=kCustom, calls=%fused_computation.11.clone | custom fusion | bytes 25166080 | tf_op jit(solution)/shard_map/jit(_take)/gather | solution.py:113
  788.7 15.9 %copy.257 = bf16[8,8,6,128,128]{3,4,2,1,0:T(8,128)(2,1)} copy(bf16[8,8,6,128,128]{4,3,2,1,0:T(8,128)(2,1)} %bitcast.150) | data formatting | bytes 25165824 | tf_op jit(solution)/shard_map/jit(_take)/gather | solution.py:113
  804.5 16.6 %copy.246 = bf16[8,8,6,128,128]{3,4,2,1,0:T(8,128)(2,1)} copy(bf16[8,8,6,128,128]{4,3,2,1,0:T(8,128)(2,1)} %bitcast.151) | data formatting | bytes 25165824 | tf_op jit(solution)/shard_map/jit(_take)/gather | solution.py:113
  848.5 17.4 %gather_fusion.7 = bf16[64,6,128,128]{3,2,1,0:T(8,128)(2,1)} fusion(bf16[160,6,128,128]{3,2,1,0:T(8,128)(2,1)} %dynamic-slice_bitcast_fusion, s32[1024]{0:T(1024)S(1)} %pad_clamp_fusion.6), kind=kCustom, calls=%fused_computation.2.clone | custom fusion | bytes 25166080 | tf_op jit(solution)/shard_map/jit(_take)/gather | solution.py:113
  865.9 17.2 %gather_fusion.16 = bf16[64,6,128,128]{3,2,1,0:T(8,128)(2,1)} fusion(bf16[160,6,128,128]{3,2,1,0:T(8,128)(2,1)} %dynamic-slice_bitcast_fusion, s32[1024]{0:T(1024)S(1)} %pad_clamp_fusion.1), kind=kCustom, calls=%fused_computation.13.clone | custom fusion | bytes 25166080 | tf_op jit(solution)/shard_map/jit(_take)/gather | solution.py:113
  883.1 24.8 %copy.258 = f32[8,8,6,128,128]{4,1,2,3,0:T(8,128)} copy(f32[8,8,6,128,128]{3,4,2,1,0:T(8,128)} %fusion.18) | data formatting | bytes 50331648 | tf_op jit(solution)/shard_map/rvab,rvsbe->rvsae/transpose | solution.py:114
  907.9 24.8 %copy.247 = f32[8,8,6,128,128]{4,1,2,3,0:T(8,128)} copy(f32[8,8,6,128,128]{3,4,2,1,0:T(8,128)} %fusion.15) | data formatting | bytes 50331648 | tf_op jit(solution)/shard_map/rvab,rvsbe->rvsae/transpose | solution.py:114
  932.7 16.6 %copy.235 = bf16[8,8,6,128,128]{3,4,2,1,0:T(8,128)(2,1)} copy(bf16[8,8,6,128,128]{4,3,2,1,0:T(8,128)(2,1)} %bitcast.149) | data formatting | bytes 25165824 | tf_op jit(solution)/shard_map/jit(_take)/gather | solution.py:113
  963.0 24.8 %copy.236 = f32[8,8,6,128,128]{4,1,2,3,0:T(8,128)} copy(f32[8,8,6,128,128]{3,4,2,1,0:T(8,128)} %fusion.12) | data formatting | bytes 50331648 | tf_op jit(solution)/shard_map/rvab,rvsbe->rvsae/transpose | solution.py:114
  987.8 16.7 %copy.268 = bf16[8,8,6,128,128]{3,4,2,1,0:T(8,128)(2,1)} copy(bf16[8,8,6,128,128]{4,3,2,1,0:T(8,128)(2,1)} %bitcast.148) | data formatting | bytes 25165824 | tf_op jit(solution)/shard_map/jit(_take)/gather | solution.py:113
  1004.4 13.7 %fusion.21 = f32[8,8,6,128,128]{3,4,2,1,0:T(8,128)} fusion(bf16[8,8,6,128,128]{3,4,2,1,0:T(8,128)(2,1)} %copy.268, pred[8,8]{1,0:T(8,128)(4,1)S(1)} %copy-done.10, bf16[8,8,128,128]{3,2,1,0:T(8,128)(2,1)} %collective-permute-done.10), kind=kOutput, calls=%fused_computation.34 | convolution fusion | flops 1616904192 | bytes 39845952 | tf_op jit(solution)/shard_map/rvab,rvsbe->rvsae/dot_general | solution.py:114
  1018.1 24.8 %copy.269 = f32[8,8,6,128,128]{4,1,2,3,0:T(8,128)} copy(f32[8,8,6,128,128]{3,4,2,1,0:T(8,128)} %fusion.21) | data formatting | bytes 50331648 | tf_op jit(solution)/shard_map/rvab,rvsbe->rvsae/transpose | solution.py:114
  1042.9 16.0 %fusion.35 = f32[8,8,128,128,1]{3,1,4,2,0:T(8,128)} fusion(f32[8,8,6,128,128]{4,1,2,3,0:T(8,128)} %copy.258, s32[8,8,6]{1,2,0:T(8,128)S(1)} %copy-done.6, s32[8,8]{1,0:T(8,128)S(1)} %copy-done.8, pred[8,8,6]{1,2,0:T(8,128)(4,1)S(1)} %copy-done.13), kind=kOutput, calls=%fused_computation.52 | convolution fusion | flops 603985920 | bytes 29362304 | tf_op jit(solution)/shard_map/ruvs,rvsae->ruae/dot_general | solution.py:117
  1058.9 15.6 %fusion.37 = f32[8,8,128,128,1]{3,1,4,2,0:T(8,128)} fusion(f32[8,8,6,128,128]{4,1,2,3,0:T(8,128)} %copy.247, s32[8,8,6]{1,2,0:T(8,128)S(1)} %copy-done.5, s32[8,8]{1,0:T(8,128)S(1)} %copy-done.8, pred[8,8,6]{1,2,0:T(8,128)(4,1)S(1)} %copy-done.12), kind=kOutput, calls=%fused_computation.54 | convolution fusion | flops 603985920 | bytes 29362304 | tf_op jit(solution)/shard_map/ruvs,rvsae->ruae/dot_general | solution.py:117
  1074.6 15.6 %fusion.39 = f32[8,8,128,128,1]{3,1,4,2,0:T(8,128)} fusion(f32[8,8,6,128,128]{4,1,2,3,0:T(8,128)} %copy.236, s32[8,8]{1,0:T(8,128)S(1)} %copy-done.8, s32[8,8,6]{1,2,0:T(8,128)S(1)} %copy-done.4, pred[8,8,6]{1,2,0:T(8,128)(4,1)S(1)} %copy-done.11), kind=kOutput, calls=%fused_computation.56 | convolution fusion | flops 603985920 | bytes 29362304 | tf_op jit(solution)/shard_map/ruvs,rvsae->ruae/dot_general | solution.py:117
  1090.2 19.6 %fusion.28 = bf16[8,8,128,128]{3,1,2,0:T(8,128)(2,1)} fusion(f32[8,8,128,128,1]{3,1,4,2,0:T(8,128)} %fusion.35, f32[8,8,128,128,1]{3,1,4,2,0:T(8,128)} %fusion.37, f32[8,8,128,128,1]{3,1,4,2,0:T(8,128)} %fusion.39, f32[8,8,6,128,128]{4,1,2,3,0:T(8,128)} %copy.269, s32[8,8,6]{1,2,0:T(8,128)S(1)} %copy-done.7, s32[8,8]{1,0:T(8,128)S(1)} %copy-done.8, ...), kind=kOutput, calls=%fused_computation.40 | convolution fusion | flops 608180224 | bytes 39848064 | tf_op jit(solution)/shard_map/ruvs,rvsae->ruae/dot_general | solution.py:117
  1110.2 18.2 %all-reduce.2.cloned.1.call-done = bf16[8,8,128,128]{3,1,2,0:T(8,128)(2,1)} async-done(((bf16[8,8,128,128]{3,1,2,0:T(8,128)(2,1)}), bf16[8,8,128,128]{3,1,2,0:T(8,128)(2,1)}) %all-reduce.2.cloned.1.call-update) | async-done | bytes 2097168 | tf_op jit(solution)/shard_map/psum | solution.py:126
  (183 shorter events, 190.0 us)
Async XLA Ops:
  6.5 192.5 %copy-start = (bf16[1,32,2,128,128]{4,3,2,1,0:T(8,128)(2,1)S(1)}, bf16[1,32,2,128,128]{4,3,2,1,0:T(8,128)(2,1)}, u32[]{:S(2)}) copy-start(bf16[1,32,2,128,128]{4,3,2,1,0:T(8,128)(2,1)} %param.15) | copy-start | bytes 6291460
  6.5 172.7 %collective-permute-start = (bf16[40,1,6,128,128]{4,3,2,1,0:T(8,128)(2,1)}, bf16[40,1,6,128,128]{4,3,2,1,0:T(8,128)(2,1)S(1)}, u32[]{:S(2)}, u32[]{:S(2)}) collective-permute-start(bf16[40,1,6,128,128]{4,3,2,1,0:T(8,128)(2,1)} %param.19), channel_id=1, source_target_pairs={{0,24},{8,0},{16,8},{24,16},{1,25},{9,1},{17,9},{25,17},{2,26},{10... | collective-permute-start | bytes 23592968 | tf_op jit(solution)/shard_map/ppermute | solution.py:14
  191.1 20.7 %copy-start.17 = (s32[40,1,6]{0,1,2:T(1,128)S(1)}, s32[40,1,6]{0,1,2:T(1,128)}, u32[]{:S(2)}) copy-start(s32[40,1,6]{0,1,2:T(1,128)} %param.21) | copy-start | bytes 2884
  191.1 494.5 %collective-permute-start.1 = (bf16[80,1,6,128,128]{4,3,2,1,0:T(8,128)(2,1)}, bf16[80,1,6,128,128]{4,3,2,1,0:T(8,128)(2,1)}, u32[]{:S(2)}, u32[]{:S(2)}) collective-permute-start(bf16[80,1,6,128,128]{4,3,2,1,0:T(8,128)(2,1)} %pad_maximum_fusion), channel_id=1, source_target_pairs={{0,16},{8,24},{16,0},{24,8},{1,17},{9,25},{17,1},{25,9},{2,18},{10... | collective-permute-start | bytes 47185928 | tf_op jit(solution)/shard_map/ppermute | solution.py:14
  193.9 10.5 all-to-all-start
  201.2 361.0 %copy-start.3 = (s32[8,1,8]{2,1,0:T(1,128)S(1)}, s32[8,1,8]{2,1,0:T(1,128)}, u32[]{:S(2)}) copy-start(s32[8,1,8]{2,1,0:T(1,128)} %param.22) | copy-start | bytes 772
  204.4 348.6 %all-to-all-start.3 = ((bf16[8,1,4,2,128,128]{5,4,3,2,1,0:T(8,128)(2,1)}), bf16[8,1,4,2,128,128]{5,4,3,2,1,0:T(8,128)(2,1)}, u32[]{:S(2)}, u32[]{:S(2)}) async-start(bf16[8,1,4,2,128,128]{5,4,3,2,1,0:T(8,128)(2,1)} %broadcast_select_fusion), calls=%async_computation.3 | async-start | bytes 4194304 | tf_op jit(solution)/shard_map/all_to_all | solution.py:57
  553.5 10.5 all-to-all-start.1
  558.4 59.5 %collective-permute-start.4 = (bf16[8,8,128,128]{3,2,1,0:T(8,128)(2,1)}, bf16[8,8,128,128]{3,2,1,0:T(8,128)(2,1)}, u32[]{:S(2)}, u32[]{:S(2)}) collective-permute-start(bf16[8,8,128,128]{3,2,1,0:T(8,128)(2,1)} %bitcast.22), channel_id=1, source_target_pairs={{0,6},{2,0},{4,2},{6,4},{1,7},{3,1},{5,3},{7,5},{8,14},{10,8},{12,... | collective-permute-start | bytes 6291464 | tf_op jit(solution)/shard_map/ppermute | solution.py:23
  564.0 44.8 %all-to-all-start.2 = ((s32[8,1,4,2]{2,3,1,0:T(2,128)}), s32[8,1,4,2]{2,3,1,0:T(2,128)S(1)}, u32[]{:S(2)}, u32[]{:S(2)}) async-start(s32[8,1,4,2]{2,3,1,0:T(2,128)} %copy.229), calls=%async_computation.2 | async-start | bytes 16384 | tf_op jit(solution)/shard_map/all_to_all | solution.py:71
  567.4 561.0 %all-reduce.2.cloned.1.call-start = ((), (), s32[]{:S(2)}) async-start(), calls=%async_computation.4 | async-start | bytes 4194304 | tf_op jit(solution)/shard_map/psum | solution.py:126
  568.2 47.3 %collective-permute-start.2 = (s32[8,8]{0,1:T(8,128)S(1)}, s32[8,8]{0,1:T(8,128)S(1)}, u32[]{:S(2)}, u32[]{:S(2)}) collective-permute-start(s32[8,8]{0,1:T(8,128)S(1)} %bitcast.164), channel_id=1, source_target_pairs={{0,6},{2,0},{4,2},{6,4},{1,7},{3,1},{5,3},{7,5},{8,14},{10,8},{12,... | collective-permute-start | bytes 776 | tf_op jit(solution)/shard_map/ppermute | solution.py:23
  609.0 8.0 collective-permute-start.3
  617.0 3.6 collective-permute-start.5
  617.9 55.5 %collective-permute-start.7 = (bf16[8,8,128,128]{3,2,1,0:T(8,128)(2,1)}, bf16[8,8,128,128]{3,2,1,0:T(8,128)(2,1)}, u32[]{:S(2)}, u32[]{:S(2)}) collective-permute-start(bf16[8,8,128,128]{3,2,1,0:T(8,128)(2,1)} %collective-permute-done.4), channel_id=1, source_target_pairs={{0,6},{2,0},{4,2},{6,4},{1,7},{3,1},{5,3},{7,5},{8,14},{10,8},{12,... | collective-permute-start | bytes 6291464 | tf_op jit(solution)/shard_map/ppermute | solution.py:23
  619.7 45.2 %collective-permute-start.6 = (s32[8,8]{0,1:T(8,128)S(1)}, s32[8,8]{0,1:T(8,128)S(1)}, u32[]{:S(2)}, u32[]{:S(2)}) collective-permute-start(s32[8,8]{0,1:T(8,128)S(1)} %collective-permute-done.3), channel_id=1, source_target_pairs={{0,6},{2,0},{4,2},{6,4},{1,7},{3,1},{5,3},{7,5},{8,14},{10,8},{12,... | collective-permute-start | bytes 776 | tf_op jit(solution)/shard_map/ppermute | solution.py:23
  665.0 3.9 collective-permute-start.8
  668.9 3.6 collective-permute-start.9
  669.2 30.2 %copy-start.9 = (pred[8,8]{1,0:T(8,128)(4,1)}, pred[8,8]{1,0:T(8,128)(4,1)S(1)}, u32[]{:S(2)}) copy-start(pred[8,8]{1,0:T(8,128)(4,1)S(1)} %copy.259) | copy-start | bytes 196
  673.4 331.0 %collective-permute-start.10 = (bf16[8,8,128,128]{3,2,1,0:T(8,128)(2,1)}, bf16[8,8,128,128]{3,2,1,0:T(8,128)(2,1)}, u32[]{:S(2)}, u32[]{:S(2)}) collective-permute-start(bf16[8,8,128,128]{3,2,1,0:T(8,128)(2,1)} %collective-permute-done.7), channel_id=1, source_target_pairs={{0,6},{2,0},{4,2},{6,4},{1,7},{3,1},{5,3},{7,5},{8,14},{10,8},{12,... | collective-permute-start | bytes 6291464 | tf_op jit(solution)/shard_map/ppermute | solution.py:23
  1018.1 24.8 %copy-start.6 = (s32[8,8,6]{1,2,0:T(8,128)S(1)}, s32[8,8,6]{1,2,0:T(8,128)}, u32[]{:S(2)}) copy-start(s32[8,8,6]{1,2,0:T(8,128)} %copy.250) | copy-start | bytes 4612
  1018.1 24.8 %copy-start.8 = (s32[8,8]{1,0:T(8,128)S(1)}, s32[8,8]{1,0:T(8,128)}, u32[]{:S(2)}) copy-start(s32[8,8]{1,0:T(8,128)} %broadcast_select_fusion.1) | copy-start | bytes 772
  1018.1 24.8 %copy-start.13 = (pred[8,8,6]{1,2,0:T(8,128)(4,1)S(1)}, pred[8,8,6]{1,2,0:T(8,128)(4,1)}, u32[]{:S(2)}) copy-start(pred[8,8,6]{1,2,0:T(8,128)(4,1)} %copy.254) | copy-start | bytes 1156
  1090.2 45.8 %copy-start.1 = (bf16[1,32,2,128,128]{4,3,2,1,0:T(8,128)(2,1)S(1)}, bf16[1,32,2,128,128]{4,3,2,1,0:T(8,128)(2,1)}, u32[]{:S(2)}) copy-start(bf16[1,32,2,128,128]{4,3,2,1,0:T(8,128)(2,1)} %param.15) | copy-start | bytes 6291460
  (14 other events, 221.4 us)
Sparse Core Ops, SparseCore 0:
  1109.9 18.4 all-reduce.1
